TPU v7x, 32 devices: a whole 2x2x4 slice. The times are simulated.
32 devices in a mesh: dp: 8 (over z, x), tm: 4 (over y, core).
Axes of the slice: x: 2, y: 2, z: 4, core: 2. Of those that a mesh axis runs over, the one named last changes fastest.
Arguments:
- clips: bfloat16 [8, 32, 16, 16, 256], P('dp', 'tm'), may hold values from -6 to 6
- frame_counts: int32 [8], P('dp'), may hold values from 5 to 32, as said below
- weight: bfloat16 [6912, 256], P('dp'), may hold values from -0.078125 to 0.078125
- gain: float32 [256], replicated, may hold values from 0.1 to 1.9
- bias: float32 [256], replicated, may hold values from -3 to 3
- cotangent: bfloat16 [8, 16, 8, 8, 256], P('dp', 'tm'), may hold values from -6 to 6
Outputs:
- output: bfloat16 [8, 16, 8, 8, 256], P('dp', 'tm')
- input_grad: bfloat16 [8, 32, 16, 16, 256], P('dp', 'tm')
- weight_grad: float32 [6912, 256], P('dp')
Inputs may be any that keep to these rules, and one draw needn't show every extreme that they name: frame_counts[c] frames of clip c are valid, the remaining slots are padding; in every draw some clip uses all 32 slots.
All inputs are finite; a program needn't handle non-finite values.
Results may differ from a plain program's by a relative error of at most 0.0048.
Values may be sent and summed in bfloat16 or wider, within the bound.
A program may use at most 64 MiB of HBM per device.

v0:
```python
import jax
import jax.numpy as jnp
from jax import lax
from jax.sharding import PartitionSpec as P

GROUPS = 32


EPS = 1e-06


def shifted(value, axis, by):
    devices = lax.axis_size(axis)
    pairs = [(i, i + by) for i in range(devices) if 0 <= i + by < devices]
    return lax.ppermute(value, axis, pairs)


def unfold(padded, frames_out, rows_out, cols_out):
    tap_list = []
    for step_t in range(3):
        for step_r in range(3):
            for step_c in range(3):
                tap_piece = padded[
                    step_t : step_t + 2 * frames_out : 2,
                    step_r : step_r + 2 * rows_out : 2,
                    step_c : step_c + 2 * cols_out : 2,
                    :,
                ]
                tap_list.append(tap_piece.reshape(frames_out * rows_out * cols_out, -1))
    return jnp.concatenate(tap_list, axis=1)


def spread_taps(values, data_axis, tap_axis, length):
    moved = jnp.moveaxis(values, tap_axis, 0)
    count = moved.shape[data_axis + 1]
    width_list = [(0, 0)] * (moved.ndim - 1)
    after = list(width_list)
    after[data_axis] = (0, 1)
    before = list(width_list)
    before[data_axis] = (1, 0)
    even_part = jnp.pad(moved[0], after) + jnp.pad(moved[2], before)
    odd_part = jnp.pad(moved[1], after)
    joined = jnp.stack([even_part, odd_part], axis=data_axis + 1)
    shape_new = list(even_part.shape)
    shape_new[data_axis] = 2 * (count + 1)
    joined = joined.reshape(shape_new)
    return lax.slice_in_dim(joined, 0, length, axis=data_axis)


def fold_back(columns, padded_shape, frames_out, rows_out, cols_out):
    channels = padded_shape[3]
    blocks = columns.reshape(frames_out, rows_out, cols_out, 3, 3, 3, channels)
    blocks = spread_taps(blocks, 0, 3, padded_shape[0])
    blocks = spread_taps(blocks, 1, 3, padded_shape[1])
    blocks = spread_taps(blocks, 2, 3, padded_shape[2])
    return blocks


def silu_slope(preact):
    sig = jax.nn.sigmoid(preact)
    return sig * (1.0 + preact * (1.0 - sig))


def shards(clips, frame_counts, weight, gain, bias, cotangent):
    clip_data = clips[0]
    cot_block = cotangent[0]
    frame_count, row_count, col_count, channels = clip_data.shape
    width_g = channels // GROUPS
    first_frame = lax.axis_index("tm") * frame_count
    frame_mask = (first_frame + jnp.arange(frame_count) < frame_counts[0]).astype(jnp.float32)[
        :, None, None, None
    ]
    mask_group = frame_mask[..., None]
    entries = frame_counts[0].astype(jnp.float32) * (row_count * col_count * width_g)
    values = clip_data.astype(jnp.float32).reshape(
        frame_count, row_count, col_count, GROUPS, width_g
    )
    sum_first, sum_second = lax.psum(
        (
            jnp.sum(values * mask_group, axis=(0, 1, 2, 4)),
            jnp.sum(values * values * mask_group, axis=(0, 1, 2, 4)),
        ),
        "tm",
    )
    group_mean = sum_first / entries
    variance = sum_second / entries - group_mean * group_mean
    inv_std = lax.rsqrt(variance + EPS)
    normed_g = (values - group_mean[:, None]) * inv_std[:, None]
    normed = normed_g.reshape(frame_count, row_count, col_count, channels)
    preact = normed * gain + bias
    hidden = (jax.nn.silu(preact) * frame_mask).astype(jnp.bfloat16)
    earlier = shifted(hidden[-2:], "tm", 1)
    padded = jnp.pad(jnp.concatenate([earlier, hidden], axis=0), ((0, 0), (1, 0), (1, 0), (0, 0)))
    frames_out, rows_out, cols_out = (frame_count // 2, row_count // 2, col_count // 2)
    patches = unfold(padded, frames_out, rows_out, cols_out)
    cot_rows = cot_block.reshape(-1, channels)
    full_weight = lax.all_gather(weight, "dp", axis=0, tiled=True)
    out_rows = jnp.dot(patches, full_weight, preferred_element_type=jnp.float32)
    out_block = out_rows.astype(jnp.bfloat16).reshape(frames_out, rows_out, cols_out, channels)
    dcols = lax.dot_general(
        cot_rows, full_weight, (((1,), (1,)), ((), ())), preferred_element_type=jnp.float32
    )
    dpad = fold_back(dcols, padded.shape, frames_out, rows_out, cols_out)
    passed = shifted(dpad[:2, 1:, 1:, :], "tm", -1)
    dlocal = dpad[2:, 1:, 1:, :]
    dhidden = jnp.concatenate([dlocal[:-2], dlocal[-2:] + passed], axis=0)
    dnormed = dhidden * frame_mask * silu_slope(preact) * gain
    grad_norm = dnormed.reshape(frame_count, row_count, col_count, GROUPS, width_g)
    back_first, back_second = lax.psum(
        (jnp.sum(grad_norm, axis=(0, 1, 2, 4)), jnp.sum(grad_norm * normed_g, axis=(0, 1, 2, 4))),
        "tm",
    )
    input_grad = (
        mask_group
        * inv_std[:, None]
        * (grad_norm - back_first[:, None] / entries - normed_g * back_second[:, None] / entries)
    )
    input_grad = input_grad.reshape(frame_count, row_count, col_count, channels).astype(
        jnp.bfloat16
    )
    local_grad = lax.dot_general(
        patches, cot_rows, (((0,), (0,)), ((), ())), preferred_element_type=jnp.float32
    )
    clip_grad = lax.psum(local_grad, "tm")
    weight_grad = lax.psum_scatter(clip_grad, "dp", scatter_dimension=0, tiled=True)
    return (out_block[None], input_grad[None], weight_grad)


def solution(mesh):
    placed = (
        P("dp", "tm", None, None, None),
        P("dp"),
        P("dp", None),
        P(),
        P(),
        P("dp", "tm", None, None, None),
    )
    return jax.shard_map(
        shards,
        mesh=mesh,
        in_specs=placed,
        out_specs=(P("dp", "tm", None, None, None), P("dp", "tm", None, None, None), P("dp", None)),
        check_vma=False,
    )
```

profile of v0, /device:TPU:0, one launch (start us, length us, event | category | flops | bytes accessed | tf_op | source)
XLA Modules:
  0.0 398.6 jit_solution(1808083092063788715)
XLA Ops:
  7.2 0.7 all-gather.2.cloned.1.call-update
  8.6 1.8 fusion.18
  10.9 8.4 %all-reduce.11 = (f32[32]{0:T(128)S(1)}, f32[32]{0:T(128)S(1)}) all-reduce(f32[32]{0:T(128)S(1)} %reduce_sum.51, f32[32]{0:T(128)S(1)} %reduce_sum.54), channel_id=1, replica_groups=mesh['dp'=8,'tm'=4] {'tm'}, use_global_device_ids=true, to_apply=%region_2.0 | all-reduce | flops 64 | bytes 512 | tf_op jit(solution)/shard_map/psum | solution.py:78
  19.6 2.1 fusion.15
  21.7 1.3 collective-permute-start
  23.0 1.1 collective-permute-done
  24.2 1.0 fusion.38
  25.2 1.2 slice.155
  26.4 1.2 slice.154
  27.6 0.9 slice.153
  28.5 0.8 slice.152
  29.3 0.8 slice.151
  30.1 0.9 slice.150
  31.0 0.8 slice.149
  31.8 0.8 slice.148
  32.6 1.5 slice.147
  34.1 9.8 %slice.146 = bf16[4,8,8,256]{3,2,1,0:T(8,128)(2,1)} slice(bf16[10,17,17,256]{3,2,1,0:T(8,128)(2,1)S(1)} %fusion.38), slice={[1:9:2], [2:17:2], [1:17:2], [0:256:1]} | slice | bytes 262144 | tf_op jit(solution)/shard_map/slice | solution.py:23
  43.9 9.7 %slice.145 = bf16[4,8,8,256]{3,2,1,0:T(8,128)(2,1)} slice(bf16[10,17,17,256]{3,2,1,0:T(8,128)(2,1)S(1)} %fusion.38), slice={[1:9:2], [2:17:2], [0:16:2], [0:256:1]} | slice | bytes 262144 | tf_op jit(solution)/shard_map/slice | solution.py:23
  53.6 9.8 %slice.144 = bf16[4,8,8,256]{3,2,1,0:T(8,128)(2,1)} slice(bf16[10,17,17,256]{3,2,1,0:T(8,128)(2,1)S(1)} %fusion.38), slice={[1:9:2], [1:17:2], [2:17:2], [0:256:1]} | slice | bytes 262144 | tf_op jit(solution)/shard_map/slice | solution.py:23
  63.4 9.7 %slice.143 = bf16[4,8,8,256]{3,2,1,0:T(8,128)(2,1)} slice(bf16[10,17,17,256]{3,2,1,0:T(8,128)(2,1)S(1)} %fusion.38), slice={[1:9:2], [1:17:2], [1:17:2], [0:256:1]} | slice | bytes 262144 | tf_op jit(solution)/shard_map/slice | solution.py:23
  73.1 9.7 %slice.142 = bf16[4,8,8,256]{3,2,1,0:T(8,128)(2,1)} slice(bf16[10,17,17,256]{3,2,1,0:T(8,128)(2,1)S(1)} %fusion.38), slice={[1:9:2], [1:17:2], [0:16:2], [0:256:1]} | slice | bytes 262144 | tf_op jit(solution)/shard_map/slice | solution.py:23
  82.8 9.7 %slice.141 = bf16[4,8,8,256]{3,2,1,0:T(8,128)(2,1)} slice(bf16[10,17,17,256]{3,2,1,0:T(8,128)(2,1)S(1)} %fusion.38), slice={[1:9:2], [0:16:2], [2:17:2], [0:256:1]} | slice | bytes 262144 | tf_op jit(solution)/shard_map/slice | solution.py:23
  92.5 9.7 %slice.140 = bf16[4,8,8,256]{3,2,1,0:T(8,128)(2,1)} slice(bf16[10,17,17,256]{3,2,1,0:T(8,128)(2,1)S(1)} %fusion.38), slice={[1:9:2], [0:16:2], [1:17:2], [0:256:1]} | slice | bytes 262144 | tf_op jit(solution)/shard_map/slice | solution.py:23
  102.2 9.7 %slice.139 = bf16[4,8,8,256]{3,2,1,0:T(8,128)(2,1)} slice(bf16[10,17,17,256]{3,2,1,0:T(8,128)(2,1)S(1)} %fusion.38), slice={[1:9:2], [0:16:2], [0:16:2], [0:256:1]} | slice | bytes 262144 | tf_op jit(solution)/shard_map/slice | solution.py:23
  111.9 9.8 %slice.138 = bf16[4,8,8,256]{3,2,1,0:T(8,128)(2,1)} slice(bf16[10,17,17,256]{3,2,1,0:T(8,128)(2,1)S(1)} %fusion.38), slice={[0:8:2], [2:17:2], [2:17:2], [0:256:1]} | slice | bytes 262144 | tf_op jit(solution)/shard_map/slice | solution.py:23
  121.7 9.7 %slice.137 = bf16[4,8,8,256]{3,2,1,0:T(8,128)(2,1)} slice(bf16[10,17,17,256]{3,2,1,0:T(8,128)(2,1)S(1)} %fusion.38), slice={[0:8:2], [2:17:2], [1:17:2], [0:256:1]} | slice | bytes 262144 | tf_op jit(solution)/shard_map/slice | solution.py:23
  131.4 9.7 %slice.136 = bf16[4,8,8,256]{3,2,1,0:T(8,128)(2,1)} slice(bf16[10,17,17,256]{3,2,1,0:T(8,128)(2,1)S(1)} %fusion.38), slice={[0:8:2], [2:17:2], [0:16:2], [0:256:1]} | slice | bytes 262144 | tf_op jit(solution)/shard_map/slice | solution.py:23
  141.1 9.8 %slice.135 = bf16[4,8,8,256]{3,2,1,0:T(8,128)(2,1)} slice(bf16[10,17,17,256]{3,2,1,0:T(8,128)(2,1)S(1)} %fusion.38), slice={[0:8:2], [1:17:2], [2:17:2], [0:256:1]} | slice | bytes 262144 | tf_op jit(solution)/shard_map/slice | solution.py:23
  150.9 9.7 %slice.134 = bf16[4,8,8,256]{3,2,1,0:T(8,128)(2,1)} slice(bf16[10,17,17,256]{3,2,1,0:T(8,128)(2,1)S(1)} %fusion.38), slice={[0:8:2], [1:17:2], [1:17:2], [0:256:1]} | slice | bytes 262144 | tf_op jit(solution)/shard_map/slice | solution.py:23
  160.6 9.7 %slice.133 = bf16[4,8,8,256]{3,2,1,0:T(8,128)(2,1)} slice(bf16[10,17,17,256]{3,2,1,0:T(8,128)(2,1)S(1)} %fusion.38), slice={[0:8:2], [1:17:2], [0:16:2], [0:256:1]} | slice | bytes 262144 | tf_op jit(solution)/shard_map/slice | solution.py:23
  170.3 9.8 %slice.132 = bf16[4,8,8,256]{3,2,1,0:T(8,128)(2,1)} slice(bf16[10,17,17,256]{3,2,1,0:T(8,128)(2,1)S(1)} %fusion.38), slice={[0:8:2], [0:16:2], [2:17:2], [0:256:1]} | slice | bytes 262144 | tf_op jit(solution)/shard_map/slice | solution.py:23
  180.1 9.7 %slice.131 = bf16[4,8,8,256]{3,2,1,0:T(8,128)(2,1)} slice(bf16[10,17,17,256]{3,2,1,0:T(8,128)(2,1)S(1)} %fusion.38), slice={[0:8:2], [0:16:2], [1:17:2], [0:256:1]} | slice | bytes 262144 | tf_op jit(solution)/shard_map/slice | solution.py:23
  189.8 9.7 %slice.130 = bf16[4,8,8,256]{3,2,1,0:T(8,128)(2,1)} slice(bf16[10,17,17,256]{3,2,1,0:T(8,128)(2,1)S(1)} %fusion.38), slice={[0:8:2], [0:16:2], [0:16:2], [0:256:1]} | slice | bytes 262144 | tf_op jit(solution)/shard_map/slice | solution.py:23
  199.6 1.5 slice.156
  201.1 1.0 constant_dynamic-update-slice_fusion.26
  202.1 0.9 constant_dynamic-update-slice_fusion.25
  203.0 0.9 constant_dynamic-update-slice_fusion.24
  203.9 0.9 constant_dynamic-update-slice_fusion.23
  204.8 0.9 constant_dynamic-update-slice_fusion.22
  205.8 0.9 constant_dynamic-update-slice_fusion.21
  206.7 0.9 constant_dynamic-update-slice_fusion.20
  207.6 0.9 constant_dynamic-update-slice_fusion.19
  208.5 0.9 constant_dynamic-update-slice_fusion.18
  209.4 0.9 constant_dynamic-update-slice_fusion.17
  210.4 0.9 constant_dynamic-update-slice_fusion.16
  211.3 0.9 constant_dynamic-update-slice_fusion.15
  212.5 1.7 copy-done.3
  214.3 4.1 %fusion.43 = f32[6912,256]{1,0:T(8,128)} fusion(bf16[256,6912]{1,0:T(8,128)(2,1)S(1)} %constant_dynamic-update-slice_fusion, bf16[256,256]{1,0:T(8,128)(2,1)S(1)} %bitcast.127), kind=kOutput, calls=%fused_computation.105 | convolution fusion | flops 905969664 | bytes 10747904 | tf_op jit(solution)/shard_map/dot_general | solution.py:121
  218.9 3.1 convolution_bitcast_fusion
  222.0 0.7 slice_bitcast_fusion.3
  224.3 0.7 slice_bitcast_fusion.6
  228.8 3.1 copy.39
  231.9 3.5 reshape.271
  235.4 1.3 slice.183
  236.7 1.5 collective-permute-start.1
  238.2 1.9 slice_bitcast_fusion.7
  240.2 3.9 convolution_convert_fusion
  244.0 1.2 fusion.39
  245.3 1.3 fusion.41
  247.1 13.6 %all-reduce.10 = (f32[32]{0:T(128)S(1)}, f32[32]{0:T(128)S(1)}) all-reduce(f32[32]{0:T(128)S(1)} %reduce_sum.75, f32[32]{0:T(128)S(1)} %reduce_sum.72), channel_id=1, replica_groups=mesh['dp'=8,'tm'=4] {'tm'}, use_global_device_ids=true, to_apply=%region_11.12 | all-reduce | flops 64 | bytes 512 | tf_op jit(solution)/shard_map/psum | solution.py:109
  261.0 92.3 %reduce-scatter.2.cloned.1.call-done = f32[864,256]{1,0:T(8,128)} async-done(((f32[6912,256]{1,0:T(8,128)}), f32[864,256]{1,0:T(8,128)}) %reduce-scatter.2.cloned.1.call-update) | async-done | bytes 884752 | tf_op jit(solution)/shard_map/reduce_scatter | solution.py:125
  353.3 1.6 fusion.37
  354.9 35.1 %all-reduce.14.cloned.1.call-done = f32[864,256]{1,0:T(8,128)} async-done(((f32[864,256]{1,0:T(8,128)}), f32[864,256]{1,0:T(8,128)}) %all-reduce.14.cloned.1.call-update) | async-done | bytes 884752 | tf_op jit(solution)/shard_map/psum | solution.py:124
  390.0 2.1 copy.76
  (80 shorter events, 7.5 us)
Async XLA Ops:
  7.2 205.4 %copy-start = (bf16[1,4,8,8,256]{4,3,2,1,0:T(8,128)(2,1)S(1)}, bf16[1,4,8,8,256]{4,3,2,1,0:T(8,128)(2,1)}, u32[]{:S(2)}) copy-start(bf16[1,4,8,8,256]{4,3,2,1,0:T(8,128)(2,1)} %param.11) | copy-start | bytes 393220
  7.2 211.7 %all-gather.2.cloned.1.call-start = ((), (), s32[]{:S(2)}) async-start(), calls=%async_computation.1 | async-start | bytes 3981312 | tf_op jit(solution)/shard_map/all_gather | solution.py:97
  7.9 345.4 %reduce-scatter.2.cloned.1.call-start = ((), (), s32[]{:S(2)}) async-start(), calls=%async_computation.2 | async-start | bytes 7962624 | tf_op jit(solution)/shard_map/reduce_scatter | solution.py:125
  21.7 2.4 collective-permute-start
  201.1 11.1 %copy-start.9 = (bf16[4,8,8,256]{3,2,1,0:T(8,128)(2,1)S(1)}, bf16[4,8,8,256]{3,2,1,0:T(8,128)(2,1)}, u32[]{:S(2)}) copy-start(bf16[4,8,8,256]{3,2,1,0:T(8,128)(2,1)} %slice.142) | copy-start | bytes 393220
  201.1 11.2 %copy-start.8 = (bf16[4,8,8,256]{3,2,1,0:T(8,128)(2,1)S(1)}, bf16[4,8,8,256]{3,2,1,0:T(8,128)(2,1)}, u32[]{:S(2)}) copy-start(bf16[4,8,8,256]{3,2,1,0:T(8,128)(2,1)} %slice.143) | copy-start | bytes 393220
  201.1 11.2 %copy-start.7 = (bf16[4,8,8,256]{3,2,1,0:T(8,128)(2,1)S(1)}, bf16[4,8,8,256]{3,2,1,0:T(8,128)(2,1)}, u32[]{:S(2)}) copy-start(bf16[4,8,8,256]{3,2,1,0:T(8,128)(2,1)} %slice.144) | copy-start | bytes 393220
  201.1 11.2 %copy-start.6 = (bf16[4,8,8,256]{3,2,1,0:T(8,128)(2,1)S(1)}, bf16[4,8,8,256]{3,2,1,0:T(8,128)(2,1)}, u32[]{:S(2)}) copy-start(bf16[4,8,8,256]{3,2,1,0:T(8,128)(2,1)} %slice.145) | copy-start | bytes 393220
  201.1 11.2 %copy-start.5 = (bf16[4,8,8,256]{3,2,1,0:T(8,128)(2,1)S(1)}, bf16[4,8,8,256]{3,2,1,0:T(8,128)(2,1)}, u32[]{:S(2)}) copy-start(bf16[4,8,8,256]{3,2,1,0:T(8,128)(2,1)} %slice.146) | copy-start | bytes 393220
  212.5 1.8 copy-start.3
  218.4 171.6 %all-reduce.14.cloned.1.call-start = ((), (), s32[]{:S(2)}) async-start(), calls=%async_computation.3 | async-start | bytes 1769472 | tf_op jit(solution)/shard_map/psum | solution.py:124
  235.4 4.8 %copy-start.4 = (bf16[256,6912]{1,0:T(8,128)(2,1)S(1)}, bf16[256,6912]{1,0:T(8,128)(2,1)}, u32[]{:S(2)}) copy-start(bf16[256,6912]{1,0:T(8,128)(2,1)} %copy-done.3) | copy-start | bytes 10616836
  236.7 7.3 %collective-permute-start.1 = (f32[2,16,16,256]{3,2,1,0:T(8,128)S(1)}, f32[2,16,16,256]{3,2,1,0:T(8,128)S(1)}, u32[]{:S(2)}, u32[]{:S(2)}) collective-permute-start(f32[2,16,16,256]{3,2,1,0:T(8,128)S(1)} %slice.183), channel_id=1, source_target_pairs={{1,0},{2,1},{3,2},{5,4},{6,5},{7,6},{9,8},{10,9},{11,10},{13,12},{... | collective-permute-start | bytes 1572872 | tf_op jit(solution)/shard_map/ppermute | solution.py:15
  240.2 5.1 %copy-start.2 = (bf16[1,8,16,16,256]{4,3,2,1,0:T(8,128)(2,1)S(1)}, bf16[1,8,16,16,256]{4,3,2,1,0:T(8,128)(2,1)}, u32[]{:S(2)}) copy-start(bf16[1,8,16,16,256]{4,3,2,1,0:T(8,128)(2,1)} %param.6) | copy-start | bytes 3145732
  240.2 5.1 %copy-start.10 = (f32[256]{0:T(256)S(1)}, f32[256]{0:T(256)}, u32[]{:S(2)}) copy-start(f32[256]{0:T(256)} %param.10) | copy-start | bytes 3076
  240.2 5.1 %copy-start.11 = (f32[256]{0:T(256)S(1)}, f32[256]{0:T(256)}, u32[]{:S(2)}) copy-start(f32[256]{0:T(256)} %param.9) | copy-start | bytes 3076
  353.3 38.8 %copy-start.1 = (bf16[1,4,8,8,256]{4,3,2,1,0:T(8,128)(2,1)S(1)}, bf16[1,4,8,8,256]{4,3,2,1,0:T(8,128)(2,1)}, u32[]{:S(2)}) copy-start(bf16[1,4,8,8,256]{4,3,2,1,0:T(8,128)(2,1)} %param.11) | copy-start | bytes 393220
Sparse Core Ops, SparseCore 0:
  10.2 67.8 all-gather.1
  218.5 134.7 reduce-scatter.1
  355.8 34.1 all-reduce.13
where the time goes:
time: 399 us
  local copies, waits for them, and re-layouts  206 us (52%)
  waiting for transfers between devices  129 us (32%)
  blocking collectives  21.9 us (5%)
  between operations  15.1 us (4%)
  other arithmetic  12.5 us (3%)
  matrix products  11 us (3%)
    slice x27, local copies, waits for them, and re-layouts, unfold(): padded[step_t:step_t + 2 * frames_out:2, step_r:step_r + 2 * rows_out:2,...  176 us
    reduce_scatter x1, waiting for transfers between devices, shards(): lax.psum_scatter(clip_grad, 'dp', scatter_dimension=0, tiled=True)  92.3 us
    psum x1, waiting for transfers between devices, shards(): clip_grad = lax.psum(local_grad, 'tm')  35.1 us
    unnamed x51, local copies, waits for them, and re-layouts  15.1 us
    psum x1, blocking collectives, shards(): lax.psum((jnp.sum(grad_norm, axis=(0, 1, 2, 4)), jnp.sum(grad_norm * norm...  13.6 us
    psum x1, blocking collectives, shards(): lax.psum((jnp.sum(values * mask_group, axis=(0, 1, 2, 4)), jnp.sum(values...  8.37 us
  transfers between devices with their start and end apart: 5, of which 3 were waited for; matrix products, arithmetic and copies ran while one was open for 57% of the time, Pallas kernels for 0%

commit v1 on v0

v1 whole, which is shorter than its diff:
```python
import functools

import jax
import jax.numpy as jnp
from jax import lax
from jax.experimental import pallas as pl
from jax.experimental.pallas import tpu as pltpu
from jax.sharding import PartitionSpec as P

GROUPS = 32
EPS = 1e-06
PARTS = 3
MESH = pl.DeviceIdType.MESH
VMEM = pl.BlockSpec(memory_space=pltpu.VMEM)
SMEM = pl.BlockSpec(memory_space=pltpu.SMEM)


def shifted(value, axis, by):
    devices = lax.axis_size(axis)
    pairs = [(i, i + by) for i in range(devices) if 0 <= i + by < devices]
    return lax.ppermute(value, axis, pairs)


def forward_kernel(place_ref, params_ref, earlier_ref, clip_ref, cot_ref, patch_ref, grad_ref, held):
    frames, half_rows, _, cols, channels = clip_ref.shape
    half_cols, lanes = cols // 2, channels // 128
    area = half_rows * half_cols
    first, valid = place_ref[0], place_ref[1]
    mean, inv_std = params_ref[0:1, :], params_ref[1:2, :]
    gain, bias = params_ref[2:3, :], params_ref[3:4, :]
    held[...] = jnp.zeros_like(held)
    for frame in range(frames + 1):
        source = earlier_ref.at[frame] if frame < 2 else clip_ref.at[frame - 2]
        slot = first + (frame - 2)
        mask = jnp.where((slot >= 0) & (slot < valid), 1.0, 0.0).astype(jnp.float32)

        def rows(index, _):
            values = source[index].astype(jnp.float32)
            preact = (values - mean) * inv_std * gain + bias
            hidden = preact / (1.0 + jnp.exp(-preact)) * mask
            for lane in range(lanes):
                part = hidden[:, :, lane * 128 : (lane + 1) * 128]
                held[lane, index, 1, 8 : 8 + cols, :] = part[0]
                held[lane, index + 1, 0, 8 : 8 + cols, :] = part[1]
            return 0

        lax.fori_loop(0, half_rows, rows, 0, unroll=2)
        for step_r in range(3):
            for step_c in range(3):
                pieces = [
                    held[
                        lane,
                        step_r // 2 : step_r // 2 + half_rows,
                        step_r % 2,
                        pl.ds(7 + step_c, half_cols, 2),
                        :,
                    ].reshape(area, 128)
                    for lane in range(lanes)
                ]
                piece = jnp.concatenate(pieces, axis=1).astype(jnp.bfloat16)
                for step_t in range(3):
                    if (frame - step_t) % 2 == 0 and 0 <= frame - step_t < frames:
                        place = (frame - step_t) // 2
                        tap = 9 * step_t + 3 * step_r + step_c
                        patch_ref[
                            place * area : (place + 1) * area,
                            tap * channels : (tap + 1) * channels,
                        ] = piece

    def tap_grad(tap, _):
        at = pl.multiple_of(tap * channels, channels)
        grad_ref[pl.ds(at, channels), :] = lax.dot_general(
            patch_ref[:, pl.ds(at, channels)],
            cot_ref[...],
            (((0,), (0,)), ((), ())),
            preferred_element_type=jnp.float32,
        )
        return 0

    lax.fori_loop(0, 27, tap_grad, 0)


def backward_kernel(
    place_ref, params_ref, patch_ref, weight_ref, cot_ref, clip_ref, out_ref, grad_ref, sums_ref, wide, views, spread
):
    frames, half_rows, _, cols, channels = clip_ref.shape
    frames_out, half_cols, lanes = frames // 2, cols // 2, channels // 128
    count = frames_out * half_rows * half_cols
    first, valid = place_ref[0], place_ref[1]
    mean, inv_std = params_ref[0:1, :], params_ref[1:2, :]
    gain, bias = params_ref[2:3, :], params_ref[3:4, :]
    total = jnp.zeros((count, channels), jnp.float32)
    depth = 9 * channels
    for step in range(3):
        total += jnp.dot(
            patch_ref[:, step * depth : (step + 1) * depth],
            weight_ref[step * depth : (step + 1) * depth, :],
            preferred_element_type=jnp.float32,
        )
    out_ref[...] = total.astype(jnp.bfloat16)
    wide[...] = jnp.zeros_like(wide)
    for frame in range(frames_out + 1):
        wide[frame, 0:half_rows, 0:half_cols, :] = cot_ref[frame].astype(jnp.float32)
    for dt in range(2):
        for dr in range(2):
            for dc in range(2):
                piece = wide[dt : dt + frames_out, dr : dr + half_rows, dc : dc + half_cols, :]
                views[4 * dt + 2 * dr + dc] = piece.reshape(count, channels).astype(jnp.bfloat16)
    times = (((2, 0), (0, 1)), ((1, 1),))
    spaces = (((1, 0),), ((2, 0), (0, 1)))
    for part_t in range(2):
        for part_r in range(2):
            for part_c in range(2):
                total = jnp.zeros((count, channels), jnp.float32)
                for step_t, dt in times[part_t]:
                    for step_r, dr in spaces[part_r]:
                        for step_c, dc in spaces[part_c]:
                            tap = 9 * step_t + 3 * step_r + step_c
                            total += lax.dot_general(
                                views[4 * dt + 2 * dr + dc],
                                weight_ref[tap * channels : (tap + 1) * channels, :],
                                (((1,), (1,)), ((), ())),
                                preferred_element_type=jnp.float32,
                            )
                total = total.reshape(frames_out, half_rows, half_cols, channels)
                for frame in range(frames_out):
                    for lane in range(lanes):
                        spread[
                            lane, 2 * frame + part_t, :, part_r, pl.ds(part_c, half_cols, 2), :
                        ] = total[frame, :, :, lane * 128 : (lane + 1) * 128]

    def rows(index, sums):
        frame, row = index // half_rows, index % half_rows
        mask = jnp.where(first + frame < valid, 1.0, 0.0).astype(jnp.float32)
        normed = (clip_ref[frame, row].astype(jnp.float32) - mean) * inv_std
        preact = normed * gain + bias
        sig = 1.0 / (1.0 + jnp.exp(-preact))
        slope = sig * (1.0 + preact * (1.0 - sig))
        hidden_grad = jnp.concatenate([spread[lane, frame, row] for lane in range(lanes)], axis=-1)
        value = hidden_grad * mask * slope * gain
        grad_ref[frame, row] = value
        return (
            sums[0] + jnp.sum(value.reshape(-1, 8, channels), axis=0),
            sums[1] + jnp.sum((value * normed).reshape(-1, 8, channels), axis=0),
        )

    zero = jnp.zeros((8, channels), jnp.float32)
    sums = lax.fori_loop(0, frames * half_rows, rows, (zero, zero), unroll=2)
    sums_ref[0] = sums[0]
    sums_ref[1] = sums[1]


def plan(dp_size, tm_size):
    dp_bits = [("dp", k) for k in range(dp_size.bit_length() - 1)]
    tm_bits = [("tm", k) for k in range(tm_size.bit_length() - 1)]
    cut = len(dp_bits) // 2
    ways = [tm_bits[1:], dp_bits[:cut], dp_bits[cut:]]
    orders = []
    for part in range(PARTS):
        turned = ways[part:] + ways[:part]
        orders.append(tm_bits[:1] + turned[0] + turned[1] + turned[2])
    return dp_bits[::-1] + tm_bits[::-1], orders


def reduce_kernel(labels, orders, grad_ref, out_ref, *scratch):
    depth = len(labels)
    sends, receives, kept = (scratch[i * depth : (i + 1) * depth] for i in range(3))
    send_sem, recv_sem, share_send, share_recv = scratch[3 * depth :]
    place = {"dp": lax.axis_index("dp"), "tm": lax.axis_index("tm")}

    def bit_of(label):
        return (place[label[0]] // 2 ** label[1]) % 2

    def partner(label):
        return {label[0]: place[label[0]] + (1 - 2 * bit_of(label)) * 2 ** label[1]}

    barrier = pltpu.get_barrier_semaphore()
    for label in labels:
        pl.semaphore_signal(barrier, inc=1, device_id=partner(label), device_id_type=MESH)
    pl.semaphore_wait(barrier, depth)

    left = [list(labels) for _ in range(PARTS)]
    copies = [[None] * depth for _ in range(PARTS)]

    def index_of(stride, number, bit):
        return (number // stride) * (2 * stride) + bit * stride + number % stride

    def read(stage, part, index):
        return grad_ref[index, part] if stage == 0 else kept[stage - 1][part, index]

    def add(stage, part):
        label = orders[part][stage]
        stride = 2 ** (len(left[part]) - 1 - left[part].index(label))
        number = 2 ** (len(left[part]) - 1)
        copies[part][stage].wait_recv()

        def one(block, _):
            kept[stage][part, block] = read(
                stage, part, index_of(stride, block, bit_of(label))
            ) + receives[stage][part, block].astype(jnp.float32)
            return 0

        lax.fori_loop(0, number, one, 0)
        left[part].remove(label)

    for stage in range(depth):
        for part in range(PARTS):
            if stage > 0:
                add(stage - 1, part)
            label = orders[part][stage]
            stride = 2 ** (len(left[part]) - 1 - left[part].index(label))
            number = 2 ** (len(left[part]) - 1)

            def pack(block, _):
                sends[stage][part, block] = read(
                    stage, part, index_of(stride, block, 1 - bit_of(label))
                ).astype(jnp.bfloat16)
                return 0

            lax.fori_loop(0, number, pack, 0)
            copies[part][stage] = pltpu.make_async_remote_copy(
                src_ref=sends[stage].at[part],
                dst_ref=receives[stage].at[part],
                send_sem=send_sem.at[part, stage],
                recv_sem=recv_sem.at[part, stage],
                device_id=partner(label),
                device_id_type=MESH,
            )
            copies[part][stage].start()
    own = place["tm"]
    for part in range(PARTS):
        add(depth - 1, part)
        out_ref[own, part] = kept[depth - 1][part, 0]

    tm_bits = [label for label in labels if label[0] == "tm"]
    shares, serial = [], 0
    for label in tm_bits:
        span = 2 ** (label[1] + 1)
        stage_shares = []
        for high in range(out_ref.shape[0] // span):
            block = high * span + own % span
            share = pltpu.make_async_remote_copy(
                src_ref=out_ref.at[block],
                dst_ref=out_ref.at[block],
                send_sem=share_send.at[serial],
                recv_sem=share_recv.at[serial],
                device_id=partner(label),
                device_id_type=MESH,
            )
            share.start()
            stage_shares.append(share)
            serial += 1
        for share in stage_shares:
            share.wait_recv()
        shares += stage_shares
    for share in shares:
        share.wait_send()
    for part in range(PARTS):
        for copy in copies[part]:
            copy.wait_send()


def reduce_grads(grads, dp_size, tm_size):
    labels, orders = plan(dp_size, tm_size)
    depth = len(labels)
    rows, channels = grads.shape
    devices = dp_size * tm_size
    piece = rows // (devices * PARTS)
    halves = [2 ** (depth - 1 - stage) for stage in range(depth)]
    half_shapes = [(PARTS, half, piece, channels) for half in halves]
    reduced = pl.pallas_call(
        functools.partial(reduce_kernel, labels, orders),
        out_shape=jax.ShapeDtypeStruct((tm_size, PARTS, piece, channels), jnp.float32),
        in_specs=[VMEM],
        out_specs=VMEM,
        scratch_shapes=[pltpu.VMEM(shape, jnp.bfloat16) for shape in half_shapes] * 2
        + [pltpu.VMEM(shape, jnp.float32) for shape in half_shapes]
        + [pltpu.SemaphoreType.DMA((PARTS, depth))] * 2
        + [pltpu.SemaphoreType.DMA((tm_size,))] * 2,
        compiler_params=pltpu.CompilerParams(
            collective_id=0, has_side_effects=True, vmem_limit_bytes=48 * 2**20
        ),
    )(grads.reshape(devices, PARTS, piece, channels))
    return reduced.reshape(rows // dp_size, channels)


def shards(dp_size, tm_size, clips, frame_counts, weight, gain, bias, cotangent):
    clip_data = clips[0]
    cot_block = cotangent[0]
    frame_count, row_count, col_count, channels = clip_data.shape
    frames_out, rows_out, cols_out = cot_block.shape[:3]
    count = frames_out * rows_out * cols_out
    width_g = channels // GROUPS
    first_frame = lax.axis_index("tm") * frame_count
    full_weight = lax.all_gather(weight, "dp", axis=0, tiled=True)
    split = (frame_count, row_count // 2, 2, col_count, channels)
    earlier = shifted(clip_data[-2:], "tm", 1).reshape((2,) + split[1:])
    cot_next = shifted(cot_block[:1], "tm", -1)
    frame_mask = (first_frame + jnp.arange(frame_count) < frame_counts[0]).astype(jnp.float32)[
        :, None, None, None
    ]
    entries = frame_counts[0].astype(jnp.float32) * (row_count * col_count * width_g)
    values = clip_data.astype(jnp.float32)
    held = values * frame_mask
    sums = jnp.stack([jnp.sum(held, axis=(0, 1, 2)), jnp.sum(held * values, axis=(0, 1, 2))])
    sums = lax.psum(jnp.sum(sums.reshape(2, GROUPS, width_g), axis=2), "tm")
    group_mean = sums[0] / entries
    variance = sums[1] / entries - group_mean * group_mean
    inv_std = lax.rsqrt(variance + EPS)
    mean_c = jnp.repeat(group_mean, width_g)
    inv_c = jnp.repeat(inv_std, width_g)
    params = jnp.concatenate([jnp.stack([mean_c, inv_c, gain, bias]), jnp.zeros((4, channels), jnp.float32)])
    place = jnp.stack([first_frame.astype(jnp.int32), frame_counts[0]])
    limit = pltpu.CompilerParams(vmem_limit_bytes=48 * 2**20)
    clip_split = clip_data.reshape(split)
    patches, grads = pl.pallas_call(
        forward_kernel,
        out_shape=(
            jax.ShapeDtypeStruct((count, 27 * channels), jnp.bfloat16),
            jax.ShapeDtypeStruct((27 * channels, channels), jnp.float32),
        ),
        in_specs=[SMEM] + [VMEM] * 4,
        out_specs=(VMEM, VMEM),
        scratch_shapes=[pltpu.VMEM((channels // 128, rows_out + 1, 2, col_count + 8, 128), jnp.float32)],
        compiler_params=limit,
    )(place, params, earlier, clip_split, cot_block.reshape(count, channels))
    weight_grad = reduce_grads(grads, dp_size, tm_size)
    output, dnormed, back = pl.pallas_call(
        backward_kernel,
        out_shape=(
            jax.ShapeDtypeStruct((count, channels), jnp.bfloat16),
            jax.ShapeDtypeStruct(split, jnp.float32),
            jax.ShapeDtypeStruct((2, 8, channels), jnp.float32),
        ),
        in_specs=[SMEM] + [VMEM] * 5,
        out_specs=(VMEM, VMEM, VMEM),
        scratch_shapes=[
            pltpu.VMEM((frames_out + 1, rows_out + 1, 16, channels), jnp.float32),
            pltpu.VMEM((8, count, channels), jnp.bfloat16),
            pltpu.VMEM((channels // 128,) + split[:-1] + (128,), jnp.float32),
        ],
        compiler_params=limit,
    )(place, params, patches, full_weight, jnp.concatenate([cot_block, cot_next]), clip_split)
    back = jnp.sum(back, axis=1).reshape(2, GROUPS, width_g)
    back = lax.psum(jnp.sum(back, axis=2), "tm") / entries
    first_c, second_c = jnp.repeat(back[0], width_g), jnp.repeat(back[1], width_g)
    normed = (values - mean_c) * inv_c
    dnormed = dnormed.reshape(clip_data.shape)
    input_grad = (frame_mask * inv_c * (dnormed - first_c - normed * second_c)).astype(jnp.bfloat16)
    return (output.reshape(cot_block.shape)[None], input_grad[None], weight_grad)


def solution(mesh):
    placed = (
        P("dp", "tm", None, None, None),
        P("dp"),
        P("dp", None),
        P(),
        P(),
        P("dp", "tm", None, None, None),
    )
    return jax.shard_map(
        functools.partial(shards, mesh.shape["dp"], mesh.shape["tm"]),
        mesh=mesh,
        in_specs=placed,
        out_specs=(P("dp", "tm", None, None, None), P("dp", "tm", None, None, None), P("dp", None)),
        check_vma=False,
    )
```

time: 399 us -> 129 us (0.32)
  local copies, waits for them, and re-layouts: 206 us -> 5.3 us
  waiting for transfers between devices: 129 us -> 0.71 us
  Pallas kernels: 0 us -> 84 us
  matrix products: 11 us -> 0 us
  blocking collectives: 21.9 us -> 14.4 us
  other arithmetic: 12.5 us -> 5.17 us
    slice x29 -> x2, local copies, waits for them, and re-layouts: 177 us -> 1.73 us  [the longest x1 0.97 us: shards(): earlier = shifted(clip_data[-2:], 'tm', 1).reshape((2,) + split[1:])]
    reduce_scatter x1 -> x0, waiting for transfers between devices: 92.3 us -> none  [shards(): lax.psum_scatter(clip_grad, 'dp', scatter_dimension=0, tiled=True)]
    pallas_call x0 -> x3, Pallas kernels: none -> 84 us  [the longest x1 64.8 us: reduce_grads(): pl.pallas_call(functools.partial(reduce_kernel, labels, orders), out_shap...]
    psum x1 -> x0, waiting for transfers between devices: 35.1 us -> none  [shards(): clip_grad = lax.psum(local_grad, 'tm')]
    unnamed x51 -> x13, local copies, waits for them, and re-layouts: 15.1 us -> 2.28 us
    dot_general x3 -> x0, matrix products: 11 us -> none  [the longest x1 4.06 us: shards(): lax.dot_general(patches, cot_rows, (((0,), (0,)), ((), ())), preferred_el...]
    psum x2, blocking collectives: 21.9 us -> 14.4 us  [the longest x1 8.32 us: shards(): sums = lax.psum(jnp.sum(sums.reshape(2, GROUPS, width_g), axis=2), 'tm')]
    another operation x5 -> x6, local copies, waits for them, and re-layouts: 4.7 us -> 0.5 us  [the longest x4 0.33 us: shards(): jnp.stack([jnp.sum(held, axis=(0, 1, 2)), jnp.sum(held * values, axis=(0,...]
  transfers between devices with their start and end apart: 5 -> 3, of which waited for: 3 -> 0; matrix products, arithmetic and copies ran while one was open for 57% -> 4% of each run, Pallas kernels for 0% -> 59%
where the time goes in v1:
time: 129 us
  Pallas kernels  84 us (65%)
  between operations  14.9 us (12%)
  blocking collectives  14.4 us (11%)
  local copies, waits for them, and re-layouts  5.3 us (4%)
  other arithmetic  5.17 us (4%)
  starting transfers between devices  4.36 us (3%)
    pallas_call x1, Pallas kernels, reduce_grads(): pl.pallas_call(functools.partial(reduce_kernel, labels, orders), out_shap...  64.8 us
    pallas_call x1, Pallas kernels, shards(): pl.pallas_call(forward_kernel, out_shape=(jax.ShapeDtypeStruct((count, 27...  11.4 us
    psum x1, blocking collectives, shards(): sums = lax.psum(jnp.sum(sums.reshape(2, GROUPS, width_g), axis=2), 'tm')  8.32 us
    pallas_call x1, Pallas kernels, shards(): pl.pallas_call(backward_kernel, out_shape=(jax.ShapeDtypeStruct((count, c...  7.76 us
    psum x1, blocking collectives, shards(): back = lax.psum(jnp.sum(back, axis=2), 'tm') / entries  6.08 us
    ppermute x2, starting transfers between devices, shifted(): return lax.ppermute(value, axis, pairs)  4.33 us
    convert_element_type x1, other arithmetic, shards(): (frame_mask * inv_c * (dnormed - first_c - normed * second_c)).astype(jnp...  3.08 us
  transfers between devices with their start and end apart: 3, of which 0 were waited for; matrix products, arithmetic and copies ran while one was open for 4% of the time, Pallas kernels for 59%

profile of v1, /device:TPU:0, one launch (start us, length us, event | category | flops | bytes accessed | tf_op | source)
XLA Modules:
  0.0 128.8 jit_solution(4099248036973999734)
XLA Ops:
  7.2 0.0 copy-start.3
  7.2 0.0 copy-start
  7.2 0.0 copy-start.5
  7.2 0.0 copy-start.4
  7.2 0.0 all-gather.2.cloned.1.call-start
  7.3 0.7 all-gather.2.cloned.1.call-update
  7.9 0.8 slice_bitcast_fusion.1
  8.7 1.3 collective-permute-start.1
  10.0 1.0 slice_bitcast_fusion
  11.0 3.0 %collective-permute-start = (bf16[2,16,16,256]{3,2,1,0:T(8,128)(2,1)S(1)}, bf16[2,16,16,256]{3,2,1,0:T(8,128)(2,1)S(1)}, u32[]{:S(2)}, u32[]{:S(2)}) collective-permute-start(bf16[2,16,16,256]{3,2,1,0:T(8,128)(2,1)S(1)} %slice_bitcast_fusion), channel_id=1, source_target_pairs={{0,1},{1,2},{2,3},{4,5},{5,6},{6,7},{8,9},{9,10},{10,11},{12,13},{... | collective-permute-start | bytes 786440 | tf_op jit(solution)/shard_map/ppermute | solution.py:21
  14.7 1.8 %multiply_reduce_fusion = (f32[256]{0:T(256)S(1)}, f32[256]{0:T(256)S(1)}) fusion(bf16[1,8,16,16,256]{4,3,2,1,0:T(8,128)(2,1)} %param.6, f32[8]{0:T(128)S(1)} %compare_convert_fusion), kind=kLoop, calls=%fused_computation.1 | loop fusion | flops 2620928 | bytes 1050656 | tf_op jit(solution)/shard_map/reduce_sum | solution.py:305
  16.5 0.1 stack.23
  16.5 0.1 copy.9
  16.6 0.1 stack.24
  16.7 0.1 copy.10
  16.8 8.3 %psum.14 = f32[2,32]{1,0:T(2,128)S(1)} all-reduce(f32[2,32]{1,0:T(2,128)S(1)} %maximum_reduce_fusion), channel_id=1, replica_groups=mesh['dp'=8,'tm'=4] {'tm'}, use_global_device_ids=true, to_apply=%region_3.0 | all-reduce | flops 64 | bytes 512 | tf_op jit(solution)/shard_map/psum | solution.py:306
  25.1 0.1 broadcast_in_dim.18
  25.2 0.1 mul.76
  25.3 0.1 broadcast_multiply_fusion
  25.4 0.1 pad_add_fusion.place_ref
  25.5 0.1 stack_reshape.7
  25.6 0.1 broadcast_in_dim.17
  25.6 0.1 sub.39
  25.7 0.1 stack_reshape.6
  25.8 0.0 copy-done.5
  25.8 0.0 copy-done.4
  25.9 0.0 collective-permute-done.1
  25.9 0.0 copy-done.3
  25.9 0.0 collective-permute-done
  25.9 0.0 copy-done
  25.9 11.4 %shard_map.85 = (bf16[256,6912]{1,0:T(8,128)(2,1)S(1)}, f32[6912,256]{1,0:T(8,128)}) custom-call(s32[2]{0:T(128)S(1)} %pad_add_fusion.place_ref, f32[8,256]{1,0:T(8,128)S(1)} %concatenate.7.params_ref, bf16[2,8,2,16,256]{4,3,2,1,0:T(8,128)(2,1)S(1)} %bitcast.45, bf16[8,8,2,16,256]{4,3,2,1,0:T(8,128)(2,1)S(1)} %bitcast.39, bf16[256,256]{1,0:T(8,128)(2,1)S(1)} %bitcast.44), custom_call_target="tpu_custom_call" | custom-call | tf_op jit(solution)/shard_map/pallas_call | solution.py:316
  37.3 0.0 copy-start.1
  37.3 64.8 %shard_map.87 = f32[4,3,72,256]{3,2,1,0:T(8,128)S(1)} custom-call(f32[32,3,72,256]{3,2,1,0:T(8,128)} %bitcast.46), custom_call_target="tpu_custom_call" | custom-call | tf_op jit(solution)/shard_map/pallas_call | solution.py:271
  102.2 0.0 copy-done.1
  102.2 0.0 all-gather.2.cloned.1.call-done.weight_ref
  102.2 7.8 %shard_map.86 = (bf16[256,256]{1,0:T(8,128)(2,1)}, f32[8,8,2,16,256]{4,3,2,1,0:T(8,128)S(1)}, f32[2,8,256]{2,1,0:T(8,128)S(1)}) custom-call(s32[2]{0:T(128)S(1)} %pad_add_fusion.place_ref, f32[8,256]{1,0:T(8,128)S(1)} %concatenate.7.params_ref, bf16[256,6912]{1,0:T(8,128)(2,1)} %copy-done.1, bf16[6912,256]{1,0:T(8,128)(2,1)} %all-gather.2.cloned.1.call-done.weight_ref, ...), custom_call_target="tpu_custom_call" | custom-call | tf_op jit(solution)/shard_map/pallas_call | solution.py:328
  110.0 0.0 copy-start.2
  110.0 1.3 %copy-done.2 = f32[8,8,2,16,256]{4,3,2,1,0:T(8,128)} copy-done((f32[8,8,2,16,256]{4,3,2,1,0:T(8,128)}, f32[8,8,2,16,256]{4,3,2,1,0:T(8,128)S(1)}, u32[]{:S(2)}) %copy-start.2) | copy-done | bytes 2097176
  111.3 0.1 reshape.79
  111.4 0.1 reduce_sum.49
  111.5 6.1 %psum.15 = f32[2,32]{1,0:T(2,128)S(1)} all-reduce(f32[2,32]{1,0:T(2,128)S(1)} %reduce_sum.49), channel_id=1, replica_groups=mesh['dp'=8,'tm'=4] {'tm'}, use_global_device_ids=true, to_apply=%region_6.0 | all-reduce | flops 64 | bytes 512 | tf_op jit(solution)/shard_map/psum | solution.py:345
  117.6 0.1 broadcast_in_dim.20
  117.7 0.1 sub.36
  117.8 0.1 broadcast_in_dim.21
  117.8 0.1 mul.82
  117.9 3.1 %fusion.4 = bf16[1,8,16,16,256]{4,3,2,1,0:T(8,128)(2,1)} fusion(bf16[1,8,16,16,256]{4,3,2,1,0:T(8,128)(2,1)S(1)} %copy-done, f32[1,8,16,16,256]{4,3,2,1,0:T(8,128)} %bitcast.42, f32[256]{0:T(256)S(1)} %mul.82, f32[256]{0:T(256)S(1)} %mul.76, f32[256]{0:T(256)S(1)} %sub.39, f32[256]{0:T(256)S(1)} %sub.36, f32[8,256]{1,0:T(8,128)S(1)} %broadcast_multiply_fusion), kind=kLoop, calls=%fused_computation.8 | loop fusion | flops 4194304 | bytes 4206592 | tf_op jit(solution)/shard_map/convert_element_type | solution.py:349
  121.0 0.9 copy.13
  (9 shorter events, 0.1 us)
Async XLA Ops:
  7.2 18.7 %copy-start.3 = (bf16[1,4,8,8,256]{4,3,2,1,0:T(8,128)(2,1)S(1)}, bf16[1,4,8,8,256]{4,3,2,1,0:T(8,128)(2,1)}, u32[]{:S(2)}) copy-start(bf16[1,4,8,8,256]{4,3,2,1,0:T(8,128)(2,1)} %param.11) | copy-start | bytes 393220
  7.2 18.8 %copy-start = (bf16[1,8,16,16,256]{4,3,2,1,0:T(8,128)(2,1)S(1)}, bf16[1,8,16,16,256]{4,3,2,1,0:T(8,128)(2,1)}, u32[]{:S(2)}) copy-start(bf16[1,8,16,16,256]{4,3,2,1,0:T(8,128)(2,1)} %param.6) | copy-start | bytes 3145732
  7.2 18.6 %copy-start.5 = (f32[256]{0:T(256)S(1)}, f32[256]{0:T(256)}, u32[]{:S(2)}) copy-start(f32[256]{0:T(256)} %param.10) | copy-start | bytes 3076
  7.2 18.6 %copy-start.4 = (f32[256]{0:T(256)S(1)}, f32[256]{0:T(256)}, u32[]{:S(2)}) copy-start(f32[256]{0:T(256)} %param.9) | copy-start | bytes 3076
  7.2 95.0 %all-gather.2.cloned.1.call-start = ((), (), s32[]{:S(2)}) async-start(), calls=%async_computation | async-start | bytes 3981312 | tf_op jit(solution)/shard_map/all_gather | solution.py:295
  8.7 17.2 %collective-permute-start.1 = (bf16[1,8,8,256]{3,2,1,0:T(8,128)(2,1)S(1)}, bf16[1,8,8,256]{3,2,1,0:T(8,128)(2,1)S(1)}, u32[]{:S(2)}, u32[]{:S(2)}) collective-permute-start(bf16[1,8,8,256]{3,2,1,0:T(8,128)(2,1)S(1)} %slice_bitcast_fusion.1), channel_id=1, source_target_pairs={{1,0},{2,1},{3,2},{5,4},{6,5},{7,6},{9,8},{10,9},{11,10},{13,12},{... | collective-permute-start | bytes 98312 | tf_op jit(solution)/shard_map/ppermute | solution.py:21
  11.0 15.0 %collective-permute-start = (bf16[2,16,16,256]{3,2,1,0:T(8,128)(2,1)S(1)}, bf16[2,16,16,256]{3,2,1,0:T(8,128)(2,1)S(1)}, u32[]{:S(2)}, u32[]{:S(2)}) collective-permute-start(bf16[2,16,16,256]{3,2,1,0:T(8,128)(2,1)S(1)} %slice_bitcast_fusion), channel_id=1, source_target_pairs={{0,1},{1,2},{2,3},{4,5},{5,6},{6,7},{8,9},{9,10},{10,11},{12,13},{... | collective-permute-start | bytes 786440 | tf_op jit(solution)/shard_map/ppermute | solution.py:21
  37.3 64.8 %copy-start.1 = (bf16[256,6912]{1,0:T(8,128)(2,1)}, bf16[256,6912]{1,0:T(8,128)(2,1)S(1)}, u32[]{:S(2)}) copy-start(bf16[256,6912]{1,0:T(8,128)(2,1)S(1)} %get-tuple-element.8.patch_ref) | copy-start | bytes 10616836
  110.0 1.4 %copy-start.2 = (f32[8,8,2,16,256]{4,3,2,1,0:T(8,128)}, f32[8,8,2,16,256]{4,3,2,1,0:T(8,128)S(1)}, u32[]{:S(2)}) copy-start(f32[8,8,2,16,256]{4,3,2,1,0:T(8,128)S(1)} %get-tuple-element.10) | copy-start | bytes 6291460
Sparse Core Ops, SparseCore 0:
  10.2 83.2 all-gather.1

commit v2 on v0

v2 whole, which is shorter than its diff:
```python
import functools

import jax
import jax.numpy as jnp
from jax import lax
from jax.experimental import pallas as pl
from jax.experimental.pallas import tpu as pltpu
from jax.sharding import PartitionSpec as P

GROUPS = 32
EPS = 1e-06
PARTS = 3
MESH = pl.DeviceIdType.MESH
VMEM = pl.BlockSpec(memory_space=pltpu.VMEM)
SMEM = pl.BlockSpec(memory_space=pltpu.SMEM)


def plan(dp_size, tm_size):
    dp_bits = [("dp", k) for k in range(dp_size.bit_length() - 1)]
    tm_bits = [("tm", k) for k in range(tm_size.bit_length() - 1)]
    cut = len(dp_bits) // 2
    ways = [tm_bits[1:], dp_bits[:cut], dp_bits[cut:]]
    orders = []
    for part in range(PARTS):
        turned = ways[part:] + ways[:part]
        orders.append(tm_bits[:1] + turned[0] + turned[1] + turned[2])
    return dp_bits[::-1] + tm_bits[::-1], orders


def lane_group_sum(value, width):
    channels = value.shape[-1]
    lane = lax.broadcasted_iota(jnp.int32, value.shape, value.ndim - 1)
    step = 1
    while step < width:
        above = pltpu.roll(value, channels - step, value.ndim - 1)
        below = pltpu.roll(value, step, value.ndim - 1)
        value = value + jnp.where((lane // step) % 2 == 0, above, below)
        step *= 2
    return value


def block_kernel(
    labels, orders, dp_size, tm_size, near, width_g,
    valid_ref, params_ref, clip_ref, cot_ref, weight_ref,
    out_ref, input_grad_ref, weight_grad_ref,
    earlier, next_cot, full_weight, patches, grads, held, wide, views, spread, moments, sums_in, back_in,
    *scratch,
):
    frames, half_rows, _, cols, channels = clip_ref.shape
    frames_out, half_cols, lanes = frames // 2, cols // 2, channels // 128
    area = half_rows * half_cols
    count = frames_out * area
    depth = len(labels)
    sends, receives, kept = (scratch[i * depth : (i + 1) * depth] for i in range(3))
    (send_sem, recv_sem, share_send, share_recv, ring_send, ring_recv, sum_send, sum_recv,
     far_send, far_recv, near_send, near_recv, mate_send, mate_recv, own_sem) = scratch[3 * depth :]
    dp, tm = lax.axis_index("dp"), lax.axis_index("tm")
    place = {"dp": dp, "tm": tm}
    far_size = dp_size // near
    far_at, near_at = dp // near, dp % near
    core = tm % 2
    mate = {"tm": tm + 1 - 2 * core}

    def bit_of(label):
        return (place[label[0]] // 2 ** label[1]) % 2

    def partner(label):
        return {label[0]: place[label[0]] + (1 - 2 * bit_of(label)) * 2 ** label[1]}

    def send(source, target, sem_out, sem_in, device):
        copy = pltpu.make_async_remote_copy(
            src_ref=source, dst_ref=target, send_sem=sem_out, recv_sem=sem_in,
            device_id=device, device_id_type=MESH,
        )
        copy.start()
        return copy

    barrier = pltpu.get_barrier_semaphore()
    greeted = [{"tm": (tm + step) % tm_size} for step in range(1, tm_size)]
    greeted += [{"dp": dp_index} for dp_index in dp_peers(dp, dp_size, near)]
    for device in greeted:
        pl.semaphore_signal(barrier, inc=1, device_id=device, device_id_type=MESH)
    pl.semaphore_wait(barrier, len(greeted))

    ring = [
        send(clip_ref.at[frames - 2 : frames], earlier, ring_send.at[0], ring_recv.at[0], {"tm": (tm + 1) % tm_size}),
        send(cot_ref.at[0:area], next_cot, ring_send.at[1], ring_recv.at[1], {"tm": (tm + tm_size - 1) % tm_size}),
    ]

    rows_w = weight_ref.shape[0]
    half_lane = pl.ds(pl.multiple_of(core * 128, 128), 128)

    def block_at(index):
        return full_weight.at[pl.ds(pl.multiple_of(index * rows_w, 8), rows_w), half_lane]

    own_copy = pltpu.make_async_copy(
        weight_ref, full_weight.at[pl.ds(pl.multiple_of(dp * rows_w, 8), rows_w), :], own_sem
    )
    own_copy.start()
    own_half = weight_ref.at[:, half_lane]
    far_copies = [
        send(own_half, block_at(dp), far_send.at[step], far_recv.at[step],
             {"dp": ((far_at + step) % far_size) * near + near_at})
        for step in range(1, far_size)
    ]
    near_copies, mate_copies = {}, []

    def send_near(step, source, index):
        for hop in range(1, near):
            near_copies[step, hop] = send(
                source, block_at(index), near_send.at[step, hop], near_recv.at[step, hop],
                {"dp": far_at * near + (near_at + hop) % near},
            )

    def send_mate(step, hop, index):
        mate_copies.append(
            send(block_at(index), block_at(index), mate_send.at[step, hop], mate_recv.at[step, hop], mate)
        )

    send_near(0, own_half, dp)

    def weight_far(step):
        far_copies[step - 1].wait_recv()
        index = ((far_at + far_size - step) % far_size) * near + near_at
        send_near(step, block_at(index), index)
        send_mate(step, 0, index)

    def weight_near(step):
        for hop in range(1, near):
            near_copies[step, hop].wait_recv()
            index = ((far_at + far_size - step) % far_size) * near + (near_at + near - hop) % near
            send_mate(step, hop, index)

    first = tm * frames
    valid = valid_ref[0]
    gain, bias = params_ref[0:1, :], params_ref[1:2, :]
    entries = jnp.full((1, channels), valid.astype(jnp.float32)) * float(2 * half_rows * cols * width_g)
    zero = jnp.zeros((8, channels), jnp.float32)

    def fold(value):
        return jnp.sum(value.reshape(-1, 8, channels), axis=0)

    def frame_mask(frame):
        slot = first + frame
        return jnp.where((slot >= 0) & (slot < valid), 1.0, 0.0).astype(jnp.float32)

    def moment_rows(index, sums):
        frame, row = index // half_rows, index % half_rows
        values = clip_ref[frame, row].astype(jnp.float32)
        masked = values * frame_mask(frame)
        return sums[0] + fold(masked), sums[1] + fold(masked * values)

    def exchange(sums, buffer, sems):
        pair = [jnp.sum(value, axis=0, keepdims=True) for value in sums]
        buffer[tm] = jnp.concatenate(pair + [jnp.zeros((6, channels), jnp.float32)], axis=0)
        copies = [
            send(buffer.at[tm], buffer.at[tm], sum_send.at[sems, step], sum_recv.at[sems, step],
                 {"tm": (tm + step) % tm_size})
            for step in range(1, tm_size)
        ]

        def finish():
            for copy in copies:
                copy.wait()
            total = buffer[0]
            for index in range(1, tm_size):
                total = total + buffer[index]
            return lane_group_sum(total, width_g)

        return finish

    finish = exchange(lax.fori_loop(0, frames * half_rows, moment_rows, (zero, zero), unroll=2), sums_in, 0)
    held[...] = jnp.zeros_like(held)
    total = finish()
    mean = total[0:1] / entries
    inv_std = lax.rsqrt(total[1:2] / entries - mean * mean + EPS)
    for copy in ring:
        copy.wait()

    ticks = [functools.partial(weight_far, step) for step in range(1, far_size)]
    for frame in range(frames + 1):
        source = earlier.at[frame] if frame < 2 else clip_ref.at[frame - 2]
        mask = frame_mask(frame - 2)

        def rows(index, _):
            values = source[index].astype(jnp.float32)
            preact = (values - mean) * inv_std * gain + bias
            hidden = preact / (1.0 + jnp.exp(-preact)) * mask
            for lane in range(lanes):
                part = hidden[:, :, lane * 128 : (lane + 1) * 128]
                held[lane, index, 1, 8 : 8 + cols, :] = part[0]
                held[lane, index + 1, 0, 8 : 8 + cols, :] = part[1]
            return 0

        lax.fori_loop(0, half_rows, rows, 0, unroll=2)
        for step_r in range(3):
            for step_c in range(3):
                pieces = [
                    held[
                        lane,
                        step_r // 2 : step_r // 2 + half_rows,
                        step_r % 2,
                        pl.ds(7 + step_c, half_cols, 2),
                        :,
                    ].reshape(area, 128)
                    for lane in range(lanes)
                ]
                piece = jnp.concatenate(pieces, axis=1).astype(jnp.bfloat16)
                for step_t in range(3):
                    if (frame - step_t) % 2 == 0 and 0 <= frame - step_t < frames:
                        at = (frame - step_t) // 2
                        tap = 9 * step_t + 3 * step_r + step_c
                        patches[at * area : (at + 1) * area, tap * channels : (tap + 1) * channels] = piece
        if frame % 3 == 2 and ticks:
            ticks.pop(0)()

    def tap_grad(tap, _):
        at = pl.multiple_of(tap * channels, channels)
        grads[pl.ds(at, channels), :] = lax.dot_general(
            patches[:, pl.ds(at, channels)],
            cot_ref[...],
            (((0,), (0,)), ((), ())),
            preferred_element_type=jnp.float32,
        )
        return 0

    lax.fori_loop(0, 27, tap_grad, 0)
    for tick in ticks:
        tick()
    for step in range(far_size):
        weight_near(step)

    left = [list(labels) for _ in range(PARTS)]
    copies = [[None] * depth for _ in range(PARTS)]
    piece_rows = grads.shape[0] // (dp_size * tm_size * PARTS)

    def index_of(stride, number, bit):
        return (number // stride) * (2 * stride) + bit * stride + number % stride

    def read(stage, part, index):
        if stage == 0:
            at = (index * PARTS + part) * piece_rows
            if piece_rows % 8 == 0:
                return grads[pl.ds(pl.multiple_of(at, 8), piece_rows), :]
            window = (piece_rows + 14) // 8 * 8
            block = grads[pl.ds(pl.multiple_of(at // 8 * 8, 8), window), :]
            return pltpu.roll(block, (window - at % 8) % window, 0)[:piece_rows]
        return kept[stage - 1][part, index]

    def add(stage, part):
        label = orders[part][stage]
        stride = 2 ** (len(left[part]) - 1 - left[part].index(label))
        number = 2 ** (len(left[part]) - 1)
        copies[part][stage].wait_recv()

        def one(block, _):
            kept[stage][part, block] = read(
                stage, part, index_of(stride, block, bit_of(label))
            ) + receives[stage][part, block].astype(jnp.float32)
            return 0

        lax.fori_loop(0, number, one, 0)
        left[part].remove(label)

    def halve(stage):
        for part in range(PARTS):
            if stage > 0:
                add(stage - 1, part)
            label = orders[part][stage]
            stride = 2 ** (len(left[part]) - 1 - left[part].index(label))
            number = 2 ** (len(left[part]) - 1)

            def pack(block, _):
                sends[stage][part, block] = read(
                    stage, part, index_of(stride, block, 1 - bit_of(label))
                ).astype(jnp.bfloat16)
                return 0

            lax.fori_loop(0, number, pack, 0)
            copies[part][stage] = send(
                sends[stage].at[part], receives[stage].at[part],
                send_sem.at[part, stage], recv_sem.at[part, stage], partner(label),
            )

    halve(0)
    for copy in mate_copies:
        copy.wait_recv()
    own_copy.wait()
    halve(1)
    total = jnp.zeros((count, channels), jnp.float32)
    deep = 9 * channels
    for step in range(3):
        total += jnp.dot(
            patches[:, step * deep : (step + 1) * deep],
            full_weight[step * deep : (step + 1) * deep, :],
            preferred_element_type=jnp.float32,
        )
    out_ref[...] = total.astype(jnp.bfloat16)
    wide[...] = jnp.zeros_like(wide)
    last = jnp.where(tm < tm_size - 1, 1.0, 0.0).astype(jnp.float32)
    for frame in range(frames_out + 1):
        if frame < frames_out:
            piece = cot_ref[frame * area : (frame + 1) * area, :].astype(jnp.float32)
        else:
            piece = next_cot[...].astype(jnp.float32) * last
        wide[frame, 0:half_rows, 0:half_cols, :] = piece.reshape(half_rows, half_cols, channels)
    for dt in range(2):
        for dr in range(2):
            for dc in range(2):
                piece = wide[dt : dt + frames_out, dr : dr + half_rows, dc : dc + half_cols, :]
                views[4 * dt + 2 * dr + dc] = piece.reshape(count, channels).astype(jnp.bfloat16)
    times = (((2, 0), (0, 1)), ((1, 1),))
    spaces = (((1, 0),), ((2, 0), (0, 1)))
    stage = 2
    for part_t in range(2):
        for part_r in range(2):
            for part_c in range(2):
                total = jnp.zeros((count, channels), jnp.float32)
                for step_t, dt in times[part_t]:
                    for step_r, dr in spaces[part_r]:
                        for step_c, dc in spaces[part_c]:
                            tap = 9 * step_t + 3 * step_r + step_c
                            total += lax.dot_general(
                                views[4 * dt + 2 * dr + dc],
                                full_weight[tap * channels : (tap + 1) * channels, :],
                                (((1,), (1,)), ((), ())),
                                preferred_element_type=jnp.float32,
                            )
                total = total.reshape(frames_out, half_rows, half_cols, channels)
                for frame in range(frames_out):
                    for lane in range(lanes):
                        spread[
                            lane, 2 * frame + part_t, :, part_r, pl.ds(part_c, half_cols, 2), :
                        ] = total[frame, :, :, lane * 128 : (lane + 1) * 128]
    halve(stage)

    def back_rows(index, sums):
        frame, row = index // half_rows, index % half_rows
        normed = (clip_ref[frame, row].astype(jnp.float32) - mean) * inv_std
        preact = normed * gain + bias
        sig = 1.0 / (1.0 + jnp.exp(-preact))
        slope = sig * (1.0 + preact * (1.0 - sig))
        hidden_grad = jnp.concatenate([spread[lane, frame, row] for lane in range(lanes)], axis=-1)
        value = hidden_grad * frame_mask(frame) * slope * gain
        for lane in range(lanes):
            spread[lane, frame, row] = value[:, :, lane * 128 : (lane + 1) * 128]
        return sums[0] + fold(value), sums[1] + fold(value * normed)

    finish = exchange(lax.fori_loop(0, frames * half_rows, back_rows, (zero, zero), unroll=2), back_in, 1)
    for stage in range(3, depth):
        halve(stage)
    for part in range(PARTS):
        add(depth - 1, part)
        weight_grad_ref[tm, part] = kept[depth - 1][part, 0]

    tm_bits = [label for label in labels if label[0] == "tm"]
    shares, serial = [], 0
    for label in tm_bits:
        span = 2 ** (label[1] + 1)
        stage_shares = []
        for high in range(tm_size // span):
            block = high * span + tm % span
            stage_shares.append(
                send(weight_grad_ref.at[block], weight_grad_ref.at[block],
                     share_send.at[serial], share_recv.at[serial], partner(label))
            )
            serial += 1
        if label == tm_bits[0]:
            total = finish()
            back_first, back_second = total[0:1] / entries, total[1:2] / entries

            def input_rows(index, _):
                frame, row = index // half_rows, index % half_rows
                normed = (clip_ref[frame, row].astype(jnp.float32) - mean) * inv_std
                value = jnp.concatenate([spread[lane, frame, row] for lane in range(lanes)], axis=-1)
                input_grad_ref[frame, row] = (
                    frame_mask(frame) * inv_std * (value - back_first - normed * back_second)
                ).astype(jnp.bfloat16)
                return 0

            lax.fori_loop(0, frames * half_rows, input_rows, 0, unroll=2)
        for share in stage_shares:
            share.wait_recv()
        shares += stage_shares
    for copy in shares + far_copies + list(near_copies.values()) + mate_copies:
        copy.wait_send()
    for part in range(PARTS):
        for copy in copies[part]:
            copy.wait_send()


def dp_peers(dp, dp_size, near):
    far_at, near_at, far_size = dp // near, dp % near, dp_size // near
    peers = [((far_at + step) % far_size) * near + near_at for step in range(1, far_size)]
    return peers + [far_at * near + (near_at + hop) % near for hop in range(1, near)]


def shards(dp_size, tm_size, clips, frame_counts, weight, gain, bias, cotangent):
    clip_data, cot_block = clips[0], cotangent[0]
    frame_count, row_count, col_count, channels = clip_data.shape
    frames_out, rows_out, cols_out = cot_block.shape[:3]
    area = rows_out * cols_out
    count = frames_out * area
    split = (frame_count, row_count // 2, 2, col_count, channels)
    labels, orders = plan(dp_size, tm_size)
    depth = len(labels)
    rows = dp_size * weight.shape[0]
    piece = rows // (dp_size * tm_size * PARTS)
    halves = [(PARTS, 2 ** (depth - 1 - stage), piece, channels) for stage in range(depth)]
    near = 2 ** ((dp_size.bit_length() - 1) // 2)
    far = dp_size // near
    lanes = channels // 128
    dma = pltpu.SemaphoreType.DMA
    f32, bf16 = jnp.float32, jnp.bfloat16
    output, input_grad, weight_grad = pl.pallas_call(
        functools.partial(block_kernel, labels, orders, dp_size, tm_size, near, channels // GROUPS),
        out_shape=(
            jax.ShapeDtypeStruct((count, channels), bf16),
            jax.ShapeDtypeStruct(split, bf16),
            jax.ShapeDtypeStruct((tm_size, PARTS, piece, channels), f32),
        ),
        in_specs=[SMEM] + [VMEM] * 4,
        out_specs=(VMEM, VMEM, VMEM),
        scratch_shapes=[
            pltpu.VMEM((2,) + split[1:], bf16),
            pltpu.VMEM((area, channels), bf16),
            pltpu.VMEM((rows, channels), bf16),
            pltpu.VMEM((count, rows), bf16),
            pltpu.VMEM((rows, channels), f32),
            pltpu.VMEM((lanes, rows_out + 1, 2, col_count + 8, 128), f32),
            pltpu.VMEM((frames_out + 1, rows_out + 1, 16, channels), f32),
            pltpu.VMEM((8, count, channels), bf16),
            pltpu.VMEM((lanes,) + split[:-1] + (128,), f32),
            pltpu.VMEM((8, channels), f32),
            pltpu.VMEM((tm_size, 8, channels), f32),
            pltpu.VMEM((tm_size, 8, channels), f32),
        ]
        + [pltpu.VMEM(shape, bf16) for shape in halves] * 2
        + [pltpu.VMEM(shape, f32) for shape in halves]
        + [dma((PARTS, depth))] * 2
        + [dma((tm_size,))] * 2
        + [dma((2,))] * 2
        + [dma((2, tm_size))] * 2
        + [dma((far,))] * 2
        + [dma((far, near))] * 4
        + [dma(())],
        compiler_params=pltpu.CompilerParams(
            collective_id=0, has_side_effects=True, vmem_limit_bytes=56 * 2**20
        ),
    )(frame_counts, jnp.stack([gain, bias]), clip_data.reshape(split), cot_block.reshape(count, channels), weight)
    return (
        output.reshape(cot_block.shape)[None],
        input_grad.reshape(clip_data.shape)[None],
        weight_grad.reshape(weight.shape),
    )


def solution(mesh):
    placed = (
        P("dp", "tm", None, None, None),
        P("dp"),
        P("dp", None),
        P(),
        P(),
        P("dp", "tm", None, None, None),
    )
    return jax.shard_map(
        functools.partial(shards, mesh.shape["dp"], mesh.shape["tm"]),
        mesh=mesh,
        in_specs=placed,
        out_specs=(P("dp", "tm", None, None, None), P("dp", "tm", None, None, None), P("dp", None)),
        check_vma=False,
    )
```

time: 399 us -> 80.2 us (0.20)
  local copies, waits for them, and re-layouts: 206 us -> 5.5 us
  waiting for transfers between devices: 129 us -> 0 us
  Pallas kernels: 0 us -> 72.3 us
  blocking collectives: 21.9 us -> 0 us
  between operations: 15.1 us -> 1.3 us
  other arithmetic: 12.5 us -> 0.58 us
  matrix products: 11 us -> 0 us
    slice x29 -> x0, local copies, waits for them, and re-layouts: 177 us -> none  [the longest x27 176 us: unfold(): padded[step_t:step_t + 2 * frames_out:2, step_r:step_r + 2 * rows_out:2,...]
    reduce_scatter x1 -> x0, waiting for transfers between devices: 92.3 us -> none  [shards(): lax.psum_scatter(clip_grad, 'dp', scatter_dimension=0, tiled=True)]
    pallas_call x0 -> x1, Pallas kernels: none -> 72.3 us  [shards(): pl.pallas_call(functools.partial(block_kernel, labels, orders, dp_size, t...]
    psum x1 -> x0, waiting for transfers between devices: 35.1 us -> none  [shards(): clip_grad = lax.psum(local_grad, 'tm')]
    psum x2 -> x0, blocking collectives: 21.9 us -> none  [the longest x1 13.6 us: shards(): lax.psum((jnp.sum(grad_norm, axis=(0, 1, 2, 4)), jnp.sum(grad_norm * norm...]
    dot_general x3 -> x0, matrix products: 11 us -> none  [the longest x1 4.06 us: shards(): lax.dot_general(patches, cot_rows, (((0,), (0,)), ((), ())), preferred_el...]
    unnamed x51 -> x9, local copies, waits for them, and re-layouts: 15.1 us -> 5.5 us
    another operation x5 -> x0, local copies, waits for them, and re-layouts: 4.7 us -> none  [spread_taps(): joined = jnp.stack([even_part, odd_part], axis=data_axis + 1)]
  transfers between devices with their start and end apart: 5 -> 0, of which waited for: 3 -> 0; matrix products, arithmetic and copies ran while one was open for 57% -> 0% of each run, Pallas kernels for 0% -> 0%
where the time goes in v2:
time: 80.2 us; the launch traced here: 79.7 us
  Pallas kernels  72.3 us (90%)
  local copies, waits for them, and re-layouts  5.5 us (7%)
  between operations  1.3 us (2%)
    pallas_call x1, Pallas kernels, shards(): pl.pallas_call(functools.partial(block_kernel, labels, orders, dp_size, t...  72.3 us
    unnamed x9, local copies, waits for them, and re-layouts  5.5 us

profile of v2, /device:TPU:0, one launch (start us, length us, event | category | flops | bytes accessed | tf_op | source)
XLA Modules:
  0.0 79.7 jit_solution(4937699820643993640)
XLA Ops:
  1.3 0.0 copy-start.2
  1.3 0.0 copy-start.1
  1.3 0.7 copy-done.2
  2.0 0.0 copy-done.1
  2.0 0.6 pad_maximum_fusion.params_ref
  2.6 72.3 %shard_map.85 = (bf16[256,256]{1,0:T(8,128)(2,1)}, bf16[8,8,2,16,256]{4,3,2,1,0:T(8,128)(2,1)}, f32[4,3,72,256]{3,2,1,0:T(8,128)}) custom-call(s32[1]{0:T(128)S(6)} %copy.12.valid_ref, f32[2,256]{1,0:T(2,128)} %pad_maximum_fusion.params_ref, bf16[8,8,2,16,256]{4,3,2,1,0:T(8,128)(2,1)} %bitcast.7, bf16[256,256]{1,0:T(8,128)(2,1)} %bitcast.10, ...), custom_call_target="tpu_custom_call" | custom-call | tf_op jit(solution)/shard_map/pallas_call | solution.py:415
  74.9 1.6 %copy.13 = bf16[1,4,8,8,256]{4,3,2,1,0:T(8,128)(2,1)} copy(bf16[1,4,8,8,256]{4,3,2,1,0:T(8,128)(2,1)} %bitcast.11) | data formatting | bytes 262144
  76.4 0.0 copy-start
  76.4 2.3 %copy.14 = bf16[1,8,16,16,256]{4,3,2,1,0:T(8,128)(2,1)} copy(bf16[1,8,16,16,256]{4,3,2,1,0:T(8,128)(2,1)} %bitcast.8) | data formatting | bytes 2097152
  78.8 0.0 copy-done
  78.8 0.9 %copy.15 = f32[864,256]{1,0:T(8,128)} copy(f32[864,256]{1,0:T(8,128)S(1)} %bitcast.9) | data formatting | bytes 1769472
Async XLA Ops:
  1.3 0.7 copy-start.2
  1.3 0.7 copy-start.1
  76.4 2.3 %copy-start = (f32[4,3,72,256]{3,2,1,0:T(8,128)S(1)}, f32[4,3,72,256]{3,2,1,0:T(8,128)}, u32[]{:S(2)}) copy-start(f32[4,3,72,256]{3,2,1,0:T(8,128)} %get-tuple-element.8) | copy-start | bytes 2654212

commit v3 on v2

--- a/solution.py
+++ b/solution.py
@@ -43,7 +43,7 @@
     labels, orders, dp_size, tm_size, near, width_g,
     valid_ref, params_ref, clip_ref, cot_ref, weight_ref,
     out_ref, input_grad_ref, weight_grad_ref,
-    earlier, next_cot, full_weight, patches, grads, held, wide, views, spread, moments, sums_in, back_in,
+    earlier, next_cot, full_weight, patches, grads, held, wide, views, spread, shared, sums_in, back_in,
     *scratch,
 ):
     frames, half_rows, _, cols, channels = clip_ref.shape
@@ -53,7 +53,7 @@
     depth = len(labels)
     sends, receives, kept = (scratch[i * depth : (i + 1) * depth] for i in range(3))
     (send_sem, recv_sem, share_send, share_recv, ring_send, ring_recv, sum_send, sum_recv,
-     far_send, far_recv, near_send, near_recv, mate_send, mate_recv, own_sem) = scratch[3 * depth :]
+     far_send, far_recv, near_send, near_recv, mate_send, mate_recv, cross_send, cross_recv, own_sem) = scratch[3 * depth :]
     dp, tm = lax.axis_index("dp"), lax.axis_index("tm")
     place = {"dp": dp, "tm": tm}
     far_size = dp_size // near
@@ -90,20 +90,30 @@
     rows_w = weight_ref.shape[0]
     half_lane = pl.ds(pl.multiple_of(core * 128, 128), 128)
 
+    crossed = tm_size == 4 and rows_w % 48 == 0
+    rows_x = rows_w // 3 if crossed else 0
+    span_w = rows_w - rows_x
+    across = (tm // 2) % 2 if crossed else 0
+    cross_mate = {"tm": (tm + 2) % tm_size}
+    span_at = across * rows_x
+
+    def rows_of(index, start, size):
+        return full_weight.at[pl.ds(pl.multiple_of(index * rows_w + start, 8), size), half_lane]
+
     def block_at(index):
-        return full_weight.at[pl.ds(pl.multiple_of(index * rows_w, 8), rows_w), half_lane]
+        return rows_of(index, span_at, span_w)
 
     own_copy = pltpu.make_async_copy(
         weight_ref, full_weight.at[pl.ds(pl.multiple_of(dp * rows_w, 8), rows_w), :], own_sem
     )
     own_copy.start()
-    own_half = weight_ref.at[:, half_lane]
+    own_half = weight_ref.at[pl.ds(pl.multiple_of(span_at, 8), span_w), half_lane]
     far_copies = [
         send(own_half, block_at(dp), far_send.at[step], far_recv.at[step],
              {"dp": ((far_at + step) % far_size) * near + near_at})
         for step in range(1, far_size)
     ]
-    near_copies, mate_copies = {}, []
+    near_copies, mate_copies, cross_copies = {}, [], []
 
     def send_near(step, source, index):
         for hop in range(1, near):
@@ -113,9 +123,21 @@
             )
 
     def send_mate(step, hop, index):
+        if crossed:
+            cross = rows_of(index, across * (span_w), rows_x)
+            copy = send(cross, cross, cross_send.at[step, hop], cross_recv.at[step, hop], cross_mate)
+            cross_copies.append((copy, step, hop, index))
         mate_copies.append(
-            send(block_at(index), block_at(index), mate_send.at[step, hop], mate_recv.at[step, hop], mate)
+            send(block_at(index), block_at(index), mate_send.at[0, step, hop], mate_recv.at[0, step, hop], mate)
         )
+
+    def weight_cross():
+        for copy, step, hop, index in cross_copies:
+            copy.wait_recv()
+            rest = rows_of(index, (1 - across) * span_w, rows_x)
+            mate_copies.append(
+                send(rest, rest, mate_send.at[1, step, hop], mate_recv.at[1, step, hop], mate)
+            )
 
     send_near(0, own_half, dp)
 
@@ -169,7 +191,7 @@
 
         return finish
 
-    finish = exchange(lax.fori_loop(0, frames * half_rows, moment_rows, (zero, zero), unroll=2), sums_in, 0)
+    finish = exchange(lax.fori_loop(0, frames * half_rows, moment_rows, (zero, zero), unroll=4), sums_in, 0)
     held[...] = jnp.zeros_like(held)
     total = finish()
     mean = total[0:1] / entries
@@ -192,7 +214,7 @@
                 held[lane, index + 1, 0, 8 : 8 + cols, :] = part[1]
             return 0
 
-        lax.fori_loop(0, half_rows, rows, 0, unroll=2)
+        lax.fori_loop(0, half_rows, rows, 0, unroll=4)
         for step_r in range(3):
             for step_c in range(3):
                 pieces = [
@@ -224,11 +246,10 @@
         )
         return 0
 
-    lax.fori_loop(0, 27, tap_grad, 0)
     for tick in ticks:
         tick()
-    for step in range(far_size):
-        weight_near(step)
+    weight_near(0)
+    lax.fori_loop(0, 27, tap_grad, 0)
 
     left = [list(labels) for _ in range(PARTS)]
     copies = [[None] * depth for _ in range(PARTS)]
@@ -283,10 +304,13 @@
             )
 
     halve(0)
+    for step in range(1, far_size):
+        weight_near(step)
+    halve(1)
+    weight_cross()
     for copy in mate_copies:
         copy.wait_recv()
     own_copy.wait()
-    halve(1)
     total = jnp.zeros((count, channels), jnp.float32)
     deep = 9 * channels
     for step in range(3):
@@ -346,12 +370,12 @@
             spread[lane, frame, row] = value[:, :, lane * 128 : (lane + 1) * 128]
         return sums[0] + fold(value), sums[1] + fold(value * normed)
 
-    finish = exchange(lax.fori_loop(0, frames * half_rows, back_rows, (zero, zero), unroll=2), back_in, 1)
+    finish = exchange(lax.fori_loop(0, frames * half_rows, back_rows, (zero, zero), unroll=4), back_in, 1)
     for stage in range(3, depth):
         halve(stage)
     for part in range(PARTS):
         add(depth - 1, part)
-        weight_grad_ref[tm, part] = kept[depth - 1][part, 0]
+        shared[tm, part] = kept[depth - 1][part, 0].astype(jnp.bfloat16)
 
     tm_bits = [label for label in labels if label[0] == "tm"]
     shares, serial = [], 0
@@ -361,7 +385,7 @@
         for high in range(tm_size // span):
             block = high * span + tm % span
             stage_shares.append(
-                send(weight_grad_ref.at[block], weight_grad_ref.at[block],
+                send(shared.at[block], shared.at[block],
                      share_send.at[serial], share_recv.at[serial], partner(label))
             )
             serial += 1
@@ -378,11 +402,13 @@
                 ).astype(jnp.bfloat16)
                 return 0
 
-            lax.fori_loop(0, frames * half_rows, input_rows, 0, unroll=2)
+            lax.fori_loop(0, frames * half_rows, input_rows, 0, unroll=4)
         for share in stage_shares:
             share.wait_recv()
         shares += stage_shares
-    for copy in shares + far_copies + list(near_copies.values()) + mate_copies:
+    for block in range(tm_size):
+        weight_grad_ref[block] = shared[block].astype(jnp.float32)
+    for copy in shares + far_copies + list(near_copies.values()) + mate_copies + [item[0] for item in cross_copies]:
         copy.wait_send()
     for part in range(PARTS):
         for copy in copies[part]:
@@ -431,7 +457,7 @@
             pltpu.VMEM((frames_out + 1, rows_out + 1, 16, channels), f32),
             pltpu.VMEM((8, count, channels), bf16),
             pltpu.VMEM((lanes,) + split[:-1] + (128,), f32),
-            pltpu.VMEM((8, channels), f32),
+            pltpu.VMEM((tm_size, PARTS, piece, channels), bf16),
             pltpu.VMEM((tm_size, 8, channels), f32),
             pltpu.VMEM((tm_size, 8, channels), f32),
         ]
@@ -442,7 +468,9 @@
         + [dma((2,))] * 2
         + [dma((2, tm_size))] * 2
         + [dma((far,))] * 2
-        + [dma((far, near))] * 4
+        + [dma((far, near))] * 2
+        + [dma((2, far, near))] * 2
+        + [dma((far, near))] * 2
         + [dma(())],
         compiler_params=pltpu.CompilerParams(
             collective_id=0, has_side_effects=True, vmem_limit_bytes=56 * 2**20

time: 80.2 us -> 71.1 us (0.89)
  Pallas kernels: 72.3 us -> 63.3 us
    pallas_call x1, Pallas kernels: 72.3 us -> 63.3 us  [shards(): pl.pallas_call(functools.partial(block_kernel, labels, orders, dp_size, t...]
where the time goes in v3:
time: 71.1 us; the launch traced here: 70.7 us
  Pallas kernels  63.3 us (89%)
  local copies, waits for them, and re-layouts  5.5 us (8%)
  between operations  1.3 us (2%)
    pallas_call x1, Pallas kernels, shards(): pl.pallas_call(functools.partial(block_kernel, labels, orders, dp_size, t...  63.3 us
    unnamed x9, local copies, waits for them, and re-layouts  5.5 us

profile of v3, /device:TPU:0, one launch (start us, length us, event | category | flops | bytes accessed | tf_op | source)
XLA Modules:
  0.0 70.7 jit_solution(2378884240252399146)
XLA Ops:
  1.3 0.0 copy-start.2
  1.3 0.0 copy-start.1
  1.3 0.7 copy-done.2
  2.0 0.0 copy-done.1
  2.0 0.6 pad_maximum_fusion.params_ref
  2.6 63.3 %shard_map.85 = (bf16[256,256]{1,0:T(8,128)(2,1)}, bf16[8,8,2,16,256]{4,3,2,1,0:T(8,128)(2,1)}, f32[4,3,72,256]{3,2,1,0:T(8,128)}) custom-call(s32[1]{0:T(128)S(6)} %copy.12.valid_ref, f32[2,256]{1,0:T(2,128)} %pad_maximum_fusion.params_ref, bf16[8,8,2,16,256]{4,3,2,1,0:T(8,128)(2,1)} %bitcast.7, bf16[256,256]{1,0:T(8,128)(2,1)} %bitcast.10, ...), custom_call_target="tpu_custom_call" | custom-call | tf_op jit(solution)/shard_map/pallas_call | solution.py:441
  65.9 1.6 %copy.13 = bf16[1,4,8,8,256]{4,3,2,1,0:T(8,128)(2,1)} copy(bf16[1,4,8,8,256]{4,3,2,1,0:T(8,128)(2,1)} %bitcast.11) | data formatting | bytes 262144
  67.4 0.0 copy-start
  67.4 2.3 %copy.14 = bf16[1,8,16,16,256]{4,3,2,1,0:T(8,128)(2,1)} copy(bf16[1,8,16,16,256]{4,3,2,1,0:T(8,128)(2,1)} %bitcast.8) | data formatting | bytes 2097152
  69.8 0.0 copy-done
  69.8 0.9 %copy.15 = f32[864,256]{1,0:T(8,128)} copy(f32[864,256]{1,0:T(8,128)S(1)} %bitcast.9) | data formatting | bytes 1769472
Async XLA Ops:
  1.3 0.7 copy-start.2
  1.3 0.7 copy-start.1
  67.4 2.3 %copy-start = (f32[4,3,72,256]{3,2,1,0:T(8,128)S(1)}, f32[4,3,72,256]{3,2,1,0:T(8,128)}, u32[]{:S(2)}) copy-start(f32[4,3,72,256]{3,2,1,0:T(8,128)} %get-tuple-element.8) | copy-start | bytes 2654212
